TPU v7x, 32 devices: a whole 2x2x4 slice. The times are simulated.
32 devices in a mesh: cuts: 2 (over core), lx: 2 (over x), ly: 8 (over z, y).
Axes of the slice: x: 2, y: 2, z: 4, core: 2. Of those that a mesh axis runs over, the one named last changes fastest.
Arguments:
- disorder: int32 [16, 16, 128], P('lx', 'ly'), may hold values from 0 to 255
- slice_bounds: float32 [12, 2], P('cuts'), may hold values from -1.5 to 1.5
- start: float32 [12, 32, 16, 16, 128], P('cuts', None, 'lx', 'ly'), may hold values from -36 to 36
- ritz: float32 [12, 8, 16, 16, 128], P('cuts', None, 'lx', 'ly'), may hold values from -4 to 4
Outputs:
- block: float32 [12, 32, 16, 16, 128], P('cuts', None, 'lx', 'ly')
- correlations: float32 [12, 16, 32], P('cuts')
All inputs are finite; a program needn't handle non-finite values.
Results may differ from a plain program's by a relative error of at most 0.000096.
Values sent between devices are 32-bit elements; how exact they have to be, the bound alone decides.
A program may use at most 64 MiB of HBM per device.

v0:
```python
import jax
import jax.numpy as jnp
from jax import lax
from jax.sharding import PartitionSpec as P

LEVELS = 256


def passed_along(value, axis, steps):
    count = lax.axis_size(axis)
    first, last = (max(0, -steps), min(count, count - steps))
    return lax.ppermute(value, axis, [(source, source + steps) for source in range(first, last)])


def padded_2(block, sides, width):
    for axis, dim in sides:
        count = lax.axis_size(axis)
        forward = [(i, i + 1) for i in range(count - 1)]
        forward.append((count - 1, 0))
        backward = [(target, source) for source, target in forward]
        low = lax.ppermute(
            lax.slice_in_dim(block, block.shape[dim] - width, None, axis=dim), axis, forward
        )
        high = lax.ppermute(lax.slice_in_dim(block, 0, width, axis=dim), axis, backward)
        block = jnp.concatenate([low, block, high], axis=dim)
    return block


def apply_scaled(field, onsite, centre):
    inner = field[:, 1:-1, 1:-1]
    beside = field[:, 2:, 1:-1] + field[:, :-2, 1:-1]
    beside = beside + field[:, 1:-1, 2:] + field[:, 1:-1, :-2]
    beside = beside + jnp.roll(inner, 1, 3) + jnp.roll(inner, -1, 3)
    return ((onsite[None] - centre) * inner - beside) / 16.0


def on_device(disorder, slice_bounds, start, ritz):
    onsite = 16.5 * (disorder.astype(jnp.float32) / jnp.float32(LEVELS - 1) - 0.5)
    count = start.shape[0]
    width = start.shape[1]
    centre = jnp.repeat((slice_bounds[:, 0] + slice_bounds[:, 1]) / 2.0, width)[:, None, None, None]
    vectors = start.reshape((count * width,) + start.shape[2:])
    lower_edge = passed_along(ritz[-1:], "cuts", 1)
    upper_edge = passed_along(ritz[:1], "cuts", -1)
    lower = jnp.concatenate([lower_edge, ritz[:-1]], 0)
    upper = jnp.concatenate([ritz[1:], upper_edge], 0)

    def filter_step(field):
        padded = padded_2(field, (("lx", 1), ("ly", 2)), 1)
        return apply_scaled(padded, onsite, centre)

    previous = vectors
    current = filter_step(vectors)
    previous, current = (current, 2.0 * filter_step(current) - previous)
    shape = current.shape
    cells = shape[1] * shape[2] * shape[3]
    total = jnp.float32(cells * lax.axis_size("lx") * lax.axis_size("ly"))
    hp = lax.Precision.HIGHEST
    filtered = current.reshape(count, width, cells)
    window = jnp.concatenate([lower, upper], 1).reshape(count, 2 * ritz.shape[1], cells)
    summed = lax.psum(jnp.einsum("src,svc->srv", window, filtered, precision=hp), ("lx", "ly"))
    correlation = summed / total
    cleaned = filtered - jnp.einsum("srv,src->svc", correlation, window, precision=hp)
    gram = lax.psum(jnp.einsum("sac,sbc->sab", cleaned, cleaned, precision=hp), ("lx", "ly"))
    factor = jnp.linalg.cholesky(gram / total)
    result = jax.scipy.linalg.solve_triangular(factor, cleaned, lower=True)
    return (result.reshape((count, width) + shape[1:]), correlation)


def solution(mesh):
    in_specs = (
        P("lx", "ly", None),
        P("cuts", None),
        P("cuts", None, "lx", "ly", None),
        P("cuts", None, "lx", "ly", None),
    )
    out_specs = (P("cuts", None, "lx", "ly", None), P("cuts", None, None))
    return jax.shard_map(
        on_device, mesh=mesh, in_specs=in_specs, out_specs=out_specs, check_vma=False
    )
```

profile of v0, /device:TPU:0, one launch (start us, length us, event | category | flops | bytes accessed | tf_op | source)
XLA Modules:
  0.0 334.0 jit_solution(6009458818156026938)
XLA Ops:
  0.6 1.1 fusion.25
  1.7 3.0 collective-permute-start
  4.7 0.1 collective-permute-start.1
  4.8 1.5 fusion.26
  6.3 2.1 collective-permute-start.8
  8.4 1.3 collective-permute-start.9
  9.7 0.8 collective-permute-done
  10.5 3.4 %collective-permute-done.1 = f32[192,1,2,128]{3,2,1,0:T(2,128)S(1)} collective-permute-done((f32[192,1,2,128]{3,2,1,0:T(2,128)S(1)}, f32[192,1,2,128]{3,2,1,0:T(2,128)S(1)}, u32[]{:S(2)}, u32[]{:S(2)}) %collective-permute-start.1) | collective-permute-done | bytes 196640 | tf_op jit(solution)/shard_map/ppermute | solution.py:21
  13.8 0.0 copy-done.3
  13.8 0.7 copy-done.5
  14.5 2.0 pad_maximum_fusion
  16.5 0.0 copy-start.10
  16.6 0.0 copy-start
  16.6 1.5 fusion.19
  18.1 4.9 %collective-permute-start.2 = (f32[192,10,1,128]{3,2,1,0:T(1,128)S(1)}, f32[192,10,1,128]{3,2,1,0:T(1,128)}, u32[]{:S(2)}, u32[]{:S(2)}) collective-permute-start(f32[192,10,1,128]{3,2,1,0:T(1,128)S(1)} %get-tuple-element.4), channel_id=1, source_target_pairs={{1,0},{2,1},{3,2},{4,3},{5,4},{6,5},{7,6},{0,7},{9,8},{10,9},{11,1... | collective-permute-start | bytes 2949128 | tf_op jit(solution)/shard_map/ppermute | solution.py:24
  23.0 0.0 collective-permute-start.3
  23.0 0.0 copy-done.10
  23.0 0.1 broadcast_in_dim.4
  23.0 0.1 sub.40
  23.1 0.7 add_multiply_fusion
  23.8 0.0 copy-done
  23.8 2.1 fusion.23
  26.0 0.0 copy-start.4
  26.0 0.0 copy-start.6
  26.0 2.1 fusion.24
  28.2 34.1 %collective-permute-done.2 = f32[192,10,1,128]{3,2,1,0:T(1,128)} collective-permute-done((f32[192,10,1,128]{3,2,1,0:T(1,128)S(1)}, f32[192,10,1,128]{3,2,1,0:T(1,128)}, u32[]{:S(2)}, u32[]{:S(2)}) %collective-permute-start.2) | collective-permute-done | bytes 983072 | tf_op jit(solution)/shard_map/ppermute | solution.py:24
  62.2 0.0 collective-permute-done.3
  62.2 0.0 copy-done.8
  62.3 0.0 copy-start.2
  62.3 9.1 %fusion.1 = f32[192,8,2,128]{3,2,1,0:T(2,128)S(1)} fusion(f32[192,8,2,128]{3,2,1,0:T(2,128)S(1)} %bitcast.24, f32[192,10,1,128]{3,2,1,0:T(1,128)} %collective-permute-done.3, f32[192,1,2,128]{3,2,1,0:T(2,128)S(1)} %copy-done.4, f32[192,1,2,128]{3,2,1,0:T(2,128)S(1)} %copy-done.6, f32[192,10,1,128]{3,2,1,0:T(1,128)} %collective-permute-done.2, ...), kind=kLoop, calls=%fused_computation.6 | loop fusion | flops 7471104 | bytes 8659712 | tf_op jit(solution)/shard_map/div | solution.py:34
  71.4 0.1 fusion.22
  71.5 1.5 collective-permute-start.4
  73.0 0.6 collective-permute-start.5
  73.6 0.2 fusion.27
  73.8 5.6 %collective-permute-done.4 = f32[192,1,2,128]{3,2,1,0:T(2,128)S(1)} collective-permute-done((f32[192,1,2,128]{3,2,1,0:T(2,128)S(1)}, f32[192,1,2,128]{3,2,1,0:T(2,128)S(1)}, u32[]{:S(2)}, u32[]{:S(2)}) %collective-permute-start.4) | collective-permute-done | bytes 196640 | tf_op jit(solution)/shard_map/ppermute | solution.py:24
  79.3 3.0 collective-permute-done.5
  82.4 0.9 pad_maximum_fusion.1
  83.3 2.8 fusion.18
  86.1 2.8 collective-permute-start.6
  88.9 0.0 collective-permute-start.7
  88.9 0.0 collective-permute-done.8
  88.9 0.0 collective-permute-done.9
  88.9 2.1 maximum_maximum_fusion
  91.0 2.6 reshape.34
  93.6 2.1 fusion.20
  95.8 0.0 copy-start.9
  95.8 2.1 fusion.21
  98.0 33.2 %collective-permute-done.6 = f32[192,10,1,128]{3,2,1,0:T(1,128)} collective-permute-done((f32[192,10,1,128]{3,2,1,0:T(1,128)}, f32[192,10,1,128]{3,2,1,0:T(1,128)}, u32[]{:S(2)}, u32[]{:S(2)}) %collective-permute-start.6) | collective-permute-done | bytes 983072 | tf_op jit(solution)/shard_map/ppermute | solution.py:24
  131.1 0.0 collective-permute-done.7
  131.1 10.1 %fusion.4 = f32[192,8,2,128]{3,2,1,0:T(2,128)} fusion(f32[192,8,2,128]{3,2,1,0:T(2,128)S(1)} %fusion.1, f32[192,10,1,128]{3,2,1,0:T(1,128)} %collective-permute-done.7, f32[192,1,2,128]{3,2,1,0:T(2,128)S(1)} %collective-permute-done.4, f32[192,1,2,128]{3,2,1,0:T(2,128)S(1)} %collective-permute-done.5, f32[192,10,1,128]{3,2,1,0:T(1,128)} %collective-permute-done.6, ...), kind=kLoop, calls=%fused_computation.9 | loop fusion | flops 7864320 | bytes 10232576 | tf_op jit(solution)/shard_map/sub | solution.py:54
  141.2 2.6 reshape.33
  143.8 1.4 fusion.28
  145.2 75.1 %psum.14 = f32[6,16,32]{2,1,0:T(8,128)S(1)} all-reduce(f32[6,16,32]{2,1,0:T(8,128)S(1)} %fusion.28), channel_id=1, replica_groups=mesh['cuts'=2,'lx'=2,'ly'=8] {'lx','ly'}, use_global_device_ids=true, to_apply=%region_0.1 | all-reduce | flops 3072 | bytes 24576 | tf_op jit(solution)/shard_map/psum | solution.py:61
  220.3 0.0 copy-start.7
  220.4 2.6 convolution_subtract_fusion
  223.0 1.5 fusion.29
  224.5 72.8 %psum.15 = f32[6,32,32]{1,2,0:T(8,128)S(1)} all-reduce(f32[6,32,32]{1,2,0:T(8,128)S(1)} %fusion.29), channel_id=1, replica_groups=mesh['cuts'=2,'lx'=2,'ly'=8] {'lx','ly'}, use_global_device_ids=true, to_apply=%region_1.2 | all-reduce | flops 6144 | bytes 49152 | tf_op jit(solution)/shard_map/psum | solution.py:64
  297.3 0.1 copy.10
  297.4 17.6 %custom-call.8 = f32[6,32,32]{2,1,0:T(8,128)S(1)} custom-call(f32[6,32,32]{2,1,0:T(8,128)S(1)} %fusion.17), custom_call_target="Cholesky" | custom-call | tf_op jit(solution)/shard_map/jit(cholesky)/cholesky | solution.py:65
  315.0 0.1 compare_reduce_fusion
  315.1 0.1 select_bitcast_fusion
  315.2 14.8 %custom-call.9 = f32[6,1,32,32]{2,3,1,0:T(8,128)S(1)} custom-call(f32[6,1,32,32]{3,2,1,0:T(8,128)S(1)} %select_bitcast_fusion), custom_call_target="InvertDiagBlocksLowerTriangular" | custom-call | tf_op jit(solution)/shard_map/jit(_solve_triangular)/vmap()/triangular_solve | solution.py:66
  330.0 1.5 fusion.15
  331.5 2.5 reshape.35
  (17 shorter events, 0.1 us)
Async XLA Ops:
  1.7 8.8 %collective-permute-start = (f32[192,1,2,128]{3,2,1,0:T(2,128)S(1)}, f32[192,1,2,128]{3,2,1,0:T(2,128)S(1)}, u32[]{:S(2)}, u32[]{:S(2)}) collective-permute-start(f32[192,1,2,128]{3,2,1,0:T(2,128)S(1)} %get-tuple-element.17), channel_id=1, source_target_pairs={{8,0},{0,8},{9,1},{1,9},{10,2},{2,10},{11,3},{3,11},{12,4},{4,12},... | collective-permute-start | bytes 589832 | tf_op jit(solution)/shard_map/ppermute | solution.py:24
  4.7 9.1 %collective-permute-start.1 = (f32[192,1,2,128]{3,2,1,0:T(2,128)S(1)}, f32[192,1,2,128]{3,2,1,0:T(2,128)S(1)}, u32[]{:S(2)}, u32[]{:S(2)}) collective-permute-start(f32[192,1,2,128]{3,2,1,0:T(2,128)S(1)} %get-tuple-element.16), channel_id=1, source_target_pairs={{0,8},{8,0},{1,9},{9,1},{2,10},{10,2},{3,11},{11,3},{4,12},{12,4},... | collective-permute-start | bytes 589832 | tf_op jit(solution)/shard_map/ppermute | solution.py:21
  6.3 82.5 %collective-permute-start.8 = (f32[1,8,8,2,128]{4,3,2,1,0:T(2,128)}, f32[1,8,8,2,128]{4,3,2,1,0:T(2,128)}, u32[]{:S(2)}, u32[]{:S(2)}) collective-permute-start(f32[1,8,8,2,128]{4,3,2,1,0:T(2,128)} %get-tuple-element.18), channel_id=1, source_target_pairs={{0,16},{1,17},{2,18},{3,19},{4,20},{5,21},{6,22},{7,23},{8,24},{9,... | collective-permute-start | bytes 196616 | tf_op jit(solution)/shard_map/ppermute | solution.py:12
  8.4 80.5 %collective-permute-start.9 = (f32[1,8,8,2,128]{4,3,2,1,0:T(2,128)}, f32[1,8,8,2,128]{4,3,2,1,0:T(2,128)}, u32[]{:S(2)}, u32[]{:S(2)}) collective-permute-start(f32[1,8,8,2,128]{4,3,2,1,0:T(2,128)} %get-tuple-element.19), channel_id=1, source_target_pairs={{16,0},{17,1},{18,2},{19,3},{20,4},{21,5},{22,6},{23,7},{24,8},{25... | collective-permute-start | bytes 196616 | tf_op jit(solution)/shard_map/ppermute | solution.py:12
  10.5 3.4 %copy-start.3 = (f32[192,1,2,128]{3,2,1,0:T(2,128)}, f32[192,1,2,128]{3,2,1,0:T(2,128)S(1)}, u32[]{:S(2)}) copy-start(f32[192,1,2,128]{3,2,1,0:T(2,128)S(1)} %collective-permute-done) | copy-start | bytes 589828
  13.8 0.7 copy-start.5
  16.5 6.4 %copy-start.10 = (f32[6,2]{0,1:T(2,128)S(1)}, f32[6,2]{0,1:T(2,128)}, u32[]{:S(2)}) copy-start(f32[6,2]{0,1:T(2,128)} %param.5) | copy-start | bytes 148
  16.6 7.3 %copy-start = (f32[6,32,8,2,128]{4,3,2,1,0:T(2,128)S(1)}, f32[6,32,8,2,128]{4,3,2,1,0:T(2,128)}, u32[]{:S(2)}) copy-start(f32[6,32,8,2,128]{4,3,2,1,0:T(2,128)} %param.6) | copy-start | bytes 4718596
  18.1 44.1 %collective-permute-start.2 = (f32[192,10,1,128]{3,2,1,0:T(1,128)S(1)}, f32[192,10,1,128]{3,2,1,0:T(1,128)}, u32[]{:S(2)}, u32[]{:S(2)}) collective-permute-start(f32[192,10,1,128]{3,2,1,0:T(1,128)S(1)} %get-tuple-element.4), channel_id=1, source_target_pairs={{1,0},{2,1},{3,2},{4,3},{5,4},{6,5},{7,6},{0,7},{9,8},{10,9},{11,1... | collective-permute-start | bytes 2949128 | tf_op jit(solution)/shard_map/ppermute | solution.py:24
  23.0 39.3 %collective-permute-start.3 = (f32[192,10,1,128]{3,2,1,0:T(1,128)S(1)}, f32[192,10,1,128]{3,2,1,0:T(1,128)}, u32[]{:S(2)}, u32[]{:S(2)}) collective-permute-start(f32[192,10,1,128]{3,2,1,0:T(1,128)S(1)} %get-tuple-element.5), channel_id=1, source_target_pairs={{0,1},{1,2},{2,3},{3,4},{4,5},{5,6},{6,7},{7,0},{8,9},{9,10},{10,1... | collective-permute-start | bytes 2949128 | tf_op jit(solution)/shard_map/ppermute | solution.py:21
  23.1 39.1 %copy-start.8 = (f32[192]{0:T(256)}, f32[192]{0:T(256)S(1)}, u32[]{:S(2)}) copy-start(f32[192]{0:T(256)S(1)} %sub.40) | copy-start | bytes 2308
  26.0 36.3 %copy-start.4 = (f32[192,1,2,128]{3,2,1,0:T(2,128)S(1)}, f32[192,1,2,128]{3,2,1,0:T(2,128)}, u32[]{:S(2)}) copy-start(f32[192,1,2,128]{3,2,1,0:T(2,128)} %copy-done.3) | copy-start | bytes 589828
  26.0 36.3 %copy-start.6 = (f32[192,1,2,128]{3,2,1,0:T(2,128)S(1)}, f32[192,1,2,128]{3,2,1,0:T(2,128)}, u32[]{:S(2)}) copy-start(f32[192,1,2,128]{3,2,1,0:T(2,128)} %copy-done.5) | copy-start | bytes 589828
  62.3 11.3 %copy-start.2 = (f32[6,8,8,2,128]{4,3,2,1,0:T(2,128)S(1)}, f32[6,8,8,2,128]{4,3,2,1,0:T(2,128)}, u32[]{:S(2)}) copy-start(f32[6,8,8,2,128]{4,3,2,1,0:T(2,128)} %param.7) | copy-start | bytes 1179652
  71.5 7.8 %collective-permute-start.4 = (f32[192,1,2,128]{3,2,1,0:T(2,128)S(1)}, f32[192,1,2,128]{3,2,1,0:T(2,128)S(1)}, u32[]{:S(2)}, u32[]{:S(2)}) collective-permute-start(f32[192,1,2,128]{3,2,1,0:T(2,128)S(1)} %get-tuple-element.11), channel_id=1, source_target_pairs={{8,0},{0,8},{9,1},{1,9},{10,2},{2,10},{11,3},{3,11},{12,4},{4,12},... | collective-permute-start | bytes 589832 | tf_op jit(solution)/shard_map/ppermute | solution.py:24
  73.0 9.4 %collective-permute-start.5 = (f32[192,1,2,128]{3,2,1,0:T(2,128)S(1)}, f32[192,1,2,128]{3,2,1,0:T(2,128)S(1)}, u32[]{:S(2)}, u32[]{:S(2)}) collective-permute-start(f32[192,1,2,128]{3,2,1,0:T(2,128)S(1)} %get-tuple-element.10), channel_id=1, source_target_pairs={{0,8},{8,0},{1,9},{9,1},{2,10},{10,2},{3,11},{11,3},{4,12},{12,4},... | collective-permute-start | bytes 589832 | tf_op jit(solution)/shard_map/ppermute | solution.py:21
  86.1 45.1 %collective-permute-start.6 = (f32[192,10,1,128]{3,2,1,0:T(1,128)}, f32[192,10,1,128]{3,2,1,0:T(1,128)}, u32[]{:S(2)}, u32[]{:S(2)}) collective-permute-start(f32[192,10,1,128]{3,2,1,0:T(1,128)} %get-tuple-element.2), channel_id=1, source_target_pairs={{1,0},{2,1},{3,2},{4,3},{5,4},{6,5},{7,6},{0,7},{9,8},{10,9},{11,1... | collective-permute-start | bytes 2949128 | tf_op jit(solution)/shard_map/ppermute | solution.py:24
  88.9 42.3 %collective-permute-start.7 = (f32[192,10,1,128]{3,2,1,0:T(1,128)}, f32[192,10,1,128]{3,2,1,0:T(1,128)}, u32[]{:S(2)}, u32[]{:S(2)}) collective-permute-start(f32[192,10,1,128]{3,2,1,0:T(1,128)} %get-tuple-element.3), channel_id=1, source_target_pairs={{0,1},{1,2},{2,3},{3,4},{4,5},{5,6},{6,7},{7,0},{8,9},{9,10},{10,1... | collective-permute-start | bytes 2949128 | tf_op jit(solution)/shard_map/ppermute | solution.py:21
  95.8 35.3 %copy-start.9 = (f32[192]{0:T(256)S(1)}, f32[192]{0:T(256)}, u32[]{:S(2)}) copy-start(f32[192]{0:T(256)} %copy-done.8) | copy-start | bytes 2308
  141.2 2.6 copy-start.1
  220.3 2.6 copy-start.7
where the time goes:
time: 335 us; the launch traced here: 334 us
  blocking collectives  148 us (44%)
  waiting for transfers between devices  80 us (24%)
  other arithmetic  57.5 us (17%)
  local copies, waits for them, and re-layouts  24.5 us (7%)
  starting transfers between devices  16.2 us (5%)
  matrix products  6.98 us (2%)
    psum x1, blocking collectives, on_device(): lax.psum(jnp.einsum('src,svc->srv', window, filtered, precision=hp), ('lx...  75.1 us
    ppermute x4, waiting for transfers between devices, padded_2(): lax.ppermute(lax.slice_in_dim(block, 0, width, axis=dim), axis, backward)  73.6 us
    psum x1, blocking collectives, on_device(): lax.psum(jnp.einsum('sac,sbc->sab', cleaned, cleaned, precision=hp), ('lx...  72.8 us
    another operation x4, other arithmetic, on_device(): factor = jnp.linalg.cholesky(gram / total)  17.7 us
    another operation x3, other arithmetic, on_device(): result = jax.scipy.linalg.solve_triangular(factor, cleaned, lower=True)  14.9 us
    ppermute x4, starting transfers between devices, padded_2(): lax.ppermute(lax.slice_in_dim(block, 0, width, axis=dim), axis, backward)  12.2 us
    sub x1, other arithmetic, on_device(): previous, current = (current, 2.0 * filter_step(current) - previous)  10.1 us
    div x1, other arithmetic, apply_scaled(): return ((onsite[None] - centre) * inner - beside) / 16.0  9.07 us
  transfers between devices with their start and end apart: 10, of which 6 were waited for; matrix products, arithmetic and copies ran while one was open for 10% of the time, Pallas kernels for 0%

commit v1 on v0

--- a/solution.py
+++ b/solution.py
@@ -58,7 +58,10 @@
     hp = lax.Precision.HIGHEST
     filtered = current.reshape(count, width, cells)
     window = jnp.concatenate([lower, upper], 1).reshape(count, 2 * ritz.shape[1], cells)
-    summed = lax.psum(jnp.einsum("src,svc->srv", window, filtered, precision=hp), ("lx", "ly"))
+    summed = jnp.sum(
+        lax.all_gather(jnp.einsum("src,svc->srv", window, filtered, precision=hp), ("lx", "ly")),
+        axis=0,
+    )
     correlation = summed / total
     cleaned = filtered - jnp.einsum("srv,src->svc", correlation, window, precision=hp)
     gram = lax.psum(jnp.einsum("sac,sbc->sab", cleaned, cleaned, precision=hp), ("lx", "ly"))

time: 335 us -> 303 us (0.904)
  blocking collectives: 148 us -> 116 us
    psum x1 -> x0, blocking collectives: 75.1 us -> none  [on_device(): lax.psum(jnp.einsum('src,svc->srv', window, filtered, precision=hp), ('lx...]
    all_gather x0 -> x1, blocking collectives: none -> 43.5 us  [on_device(): lax.all_gather(jnp.einsum('src,svc->srv', window, filtered, precision=hp)...]
  transfers between devices with their start and end apart: 10 -> 10, of which waited for: 6 -> 6; matrix products, arithmetic and copies ran while one was open for 10% -> 11% of each run, Pallas kernels for 0% -> 0%
where the time goes in v1:
time: 303 us; the launch traced here: 302 us
  blocking collectives  116 us (38%)
  waiting for transfers between devices  80 us (26%)
  other arithmetic  57.6 us (19%)
  local copies, waits for them, and re-layouts  24.5 us (8%)
  starting transfers between devices  16.2 us (5%)
  matrix products  6.98 us (2%)
    ppermute x4, waiting for transfers between devices, padded_2(): lax.ppermute(lax.slice_in_dim(block, 0, width, axis=dim), axis, backward)  73.6 us
    psum x1, blocking collectives, on_device(): lax.psum(jnp.einsum('sac,sbc->sab', cleaned, cleaned, precision=hp), ('lx...  72.8 us
    all_gather x1, blocking collectives, on_device(): lax.all_gather(jnp.einsum('src,svc->srv', window, filtered, precision=hp)...  43.5 us
    another operation x4, other arithmetic, on_device(): factor = jnp.linalg.cholesky(gram / total)  17.7 us
    another operation x3, other arithmetic, on_device(): result = jax.scipy.linalg.solve_triangular(factor, cleaned, lower=True)  14.9 us
    ppermute x4, starting transfers between devices, padded_2(): lax.ppermute(lax.slice_in_dim(block, 0, width, axis=dim), axis, backward)  12.2 us
    sub x1, other arithmetic, on_device(): previous, current = (current, 2.0 * filter_step(current) - previous)  10.1 us
    div x1, other arithmetic, apply_scaled(): return ((onsite[None] - centre) * inner - beside) / 16.0  9.07 us
  transfers between devices with their start and end apart: 10, of which 6 were waited for; matrix products, arithmetic and copies ran while one was open for 11% of the time, Pallas kernels for 0%

profile of v1, /device:TPU:0, one launch (start us, length us, event | category | flops | bytes accessed | tf_op | source)
XLA Modules:
  0.0 302.4 jit_solution(2581995156918181663)
XLA Ops:
  0.6 1.1 fusion.25
  1.7 3.0 %collective-permute-start = (f32[192,1,2,128]{3,2,1,0:T(2,128)S(1)}, f32[192,1,2,128]{3,2,1,0:T(2,128)S(1)}, u32[]{:S(2)}, u32[]{:S(2)}) collective-permute-start(f32[192,1,2,128]{3,2,1,0:T(2,128)S(1)} %get-tuple-element.17), channel_id=1, source_target_pairs={{8,0},{0,8},{9,1},{1,9},{10,2},{2,10},{11,3},{3,11},{12,4},{4,12},... | collective-permute-start | bytes 589832 | tf_op jit(solution)/shard_map/ppermute | solution.py:24
  4.7 0.1 collective-permute-start.1
  4.8 1.5 fusion.26
  6.3 2.1 collective-permute-start.8
  8.4 1.3 collective-permute-start.9
  9.7 0.8 collective-permute-done
  10.5 3.4 %collective-permute-done.1 = f32[192,1,2,128]{3,2,1,0:T(2,128)S(1)} collective-permute-done((f32[192,1,2,128]{3,2,1,0:T(2,128)S(1)}, f32[192,1,2,128]{3,2,1,0:T(2,128)S(1)}, u32[]{:S(2)}, u32[]{:S(2)}) %collective-permute-start.1) | collective-permute-done | bytes 196640 | tf_op jit(solution)/shard_map/ppermute | solution.py:21
  13.8 0.0 copy-done.3
  13.8 0.7 copy-done.5
  14.5 2.0 pad_maximum_fusion
  16.5 0.0 copy-start.10
  16.6 0.0 copy-start
  16.6 1.5 fusion.19
  18.1 4.9 %collective-permute-start.2 = (f32[192,10,1,128]{3,2,1,0:T(1,128)S(1)}, f32[192,10,1,128]{3,2,1,0:T(1,128)}, u32[]{:S(2)}, u32[]{:S(2)}) collective-permute-start(f32[192,10,1,128]{3,2,1,0:T(1,128)S(1)} %get-tuple-element.4), channel_id=1, source_target_pairs={{1,0},{2,1},{3,2},{4,3},{5,4},{6,5},{7,6},{0,7},{9,8},{10,9},{11,1... | collective-permute-start | bytes 2949128 | tf_op jit(solution)/shard_map/ppermute | solution.py:24
  23.0 0.0 collective-permute-start.3
  23.0 0.0 copy-done.10
  23.0 0.1 broadcast_in_dim.4
  23.0 0.1 sub.40
  23.1 0.7 add_multiply_fusion
  23.8 0.0 copy-done
  23.8 2.1 fusion.23
  26.0 0.0 copy-start.4
  26.0 2.1 fusion.24
  28.2 34.1 %collective-permute-done.2 = f32[192,10,1,128]{3,2,1,0:T(1,128)} collective-permute-done((f32[192,10,1,128]{3,2,1,0:T(1,128)S(1)}, f32[192,10,1,128]{3,2,1,0:T(1,128)}, u32[]{:S(2)}, u32[]{:S(2)}) %collective-permute-start.2) | collective-permute-done | bytes 983072 | tf_op jit(solution)/shard_map/ppermute | solution.py:24
  62.2 0.0 collective-permute-done.3
  62.2 0.0 copy-done.8
  62.3 0.0 copy-start.2
  62.3 9.1 %fusion.1 = f32[192,8,2,128]{3,2,1,0:T(2,128)S(1)} fusion(f32[192,8,2,128]{3,2,1,0:T(2,128)S(1)} %bitcast.25, f32[192,10,1,128]{3,2,1,0:T(1,128)} %collective-permute-done.3, f32[192,1,2,128]{3,2,1,0:T(2,128)S(1)} %copy-done.4, f32[192,1,2,128]{3,2,1,0:T(2,128)S(1)} %copy-done.6, f32[192,10,1,128]{3,2,1,0:T(1,128)} %collective-permute-done.2, ...), kind=kLoop, calls=%fused_computation.6 | loop fusion | flops 7471104 | bytes 8659712 | tf_op jit(solution)/shard_map/div | solution.py:34
  71.4 0.1 fusion.22
  71.5 1.5 collective-permute-start.4
  73.0 0.6 collective-permute-start.5
  73.6 0.2 fusion.27
  73.8 5.6 %collective-permute-done.4 = f32[192,1,2,128]{3,2,1,0:T(2,128)S(1)} collective-permute-done((f32[192,1,2,128]{3,2,1,0:T(2,128)S(1)}, f32[192,1,2,128]{3,2,1,0:T(2,128)S(1)}, u32[]{:S(2)}, u32[]{:S(2)}) %collective-permute-start.4) | collective-permute-done | bytes 196640 | tf_op jit(solution)/shard_map/ppermute | solution.py:24
  79.3 3.0 %collective-permute-done.5 = f32[192,1,2,128]{3,2,1,0:T(2,128)S(1)} collective-permute-done((f32[192,1,2,128]{3,2,1,0:T(2,128)S(1)}, f32[192,1,2,128]{3,2,1,0:T(2,128)S(1)}, u32[]{:S(2)}, u32[]{:S(2)}) %collective-permute-start.5) | collective-permute-done | bytes 196640 | tf_op jit(solution)/shard_map/ppermute | solution.py:21
  82.4 0.9 pad_maximum_fusion.1
  83.3 2.8 fusion.18
  86.1 2.8 collective-permute-start.6
  88.9 0.0 collective-permute-start.7
  88.9 0.0 collective-permute-done.8
  88.9 0.0 collective-permute-done.9
  88.9 2.1 maximum_maximum_fusion
  91.0 2.6 reshape.34
  93.6 2.1 fusion.20
  95.8 0.0 copy-start.9
  95.8 2.1 fusion.21
  98.0 33.2 %collective-permute-done.6 = f32[192,10,1,128]{3,2,1,0:T(1,128)} collective-permute-done((f32[192,10,1,128]{3,2,1,0:T(1,128)}, f32[192,10,1,128]{3,2,1,0:T(1,128)}, u32[]{:S(2)}, u32[]{:S(2)}) %collective-permute-start.6) | collective-permute-done | bytes 983072 | tf_op jit(solution)/shard_map/ppermute | solution.py:24
  131.1 0.0 collective-permute-done.7
  131.1 10.1 %fusion.4 = f32[192,8,2,128]{3,2,1,0:T(2,128)} fusion(f32[192,8,2,128]{3,2,1,0:T(2,128)S(1)} %fusion.1, f32[192,10,1,128]{3,2,1,0:T(1,128)} %collective-permute-done.7, f32[192,1,2,128]{3,2,1,0:T(2,128)S(1)} %collective-permute-done.4, f32[192,1,2,128]{3,2,1,0:T(2,128)S(1)} %collective-permute-done.5, f32[192,10,1,128]{3,2,1,0:T(1,128)} %collective-permute-done.6, ...), kind=kLoop, calls=%fused_computation.9 | loop fusion | flops 7864320 | bytes 10232576 | tf_op jit(solution)/shard_map/sub | solution.py:54
  141.2 2.6 reshape.33
  143.8 1.4 fusion.28
  145.2 43.5 %all-gather = f32[96,16,32]{2,1,0:T(8,128)S(1)} all-gather(f32[6,16,32]{2,1,0:T(8,128)S(1)} %fusion.28), channel_id=2, replica_groups=mesh['cuts'=2,'lx'=2,'ly'=8] {'lx','ly'}, dimensions={0}, use_global_device_ids=true | all-gather | bytes 208896 | tf_op jit(solution)/shard_map/all_gather | solution.py:62
  188.7 0.1 reduce_sum.9
  188.8 0.0 copy-start.7
  188.8 2.6 convolution_subtract_fusion
  191.4 1.5 fusion.29
  192.9 72.8 %psum.7 = f32[6,32,32]{1,2,0:T(8,128)S(1)} all-reduce(f32[6,32,32]{1,2,0:T(8,128)S(1)} %fusion.29), channel_id=1, replica_groups=mesh['cuts'=2,'lx'=2,'ly'=8] {'lx','ly'}, use_global_device_ids=true, to_apply=%region_1.2 | all-reduce | flops 6144 | bytes 49152 | tf_op jit(solution)/shard_map/psum | solution.py:67
  265.7 0.1 copy.13
  265.8 17.6 %custom-call.8 = f32[6,32,32]{2,1,0:T(8,128)S(1)} custom-call(f32[6,32,32]{2,1,0:T(8,128)S(1)} %fusion.17), custom_call_target="Cholesky" | custom-call | tf_op jit(solution)/shard_map/jit(cholesky)/cholesky | solution.py:68
  283.4 0.1 compare_reduce_fusion
  283.5 0.1 select_bitcast_fusion
  283.6 14.8 %custom-call.9 = f32[6,1,32,32]{2,3,1,0:T(8,128)S(1)} custom-call(f32[6,1,32,32]{3,2,1,0:T(8,128)S(1)} %select_bitcast_fusion), custom_call_target="InvertDiagBlocksLowerTriangular" | custom-call | tf_op jit(solution)/shard_map/jit(_solve_triangular)/vmap()/triangular_solve | solution.py:69
  298.4 1.5 fusion.15
  299.9 2.5 reshape.35
  (18 shorter events, 0.1 us)
Async XLA Ops:
  1.7 8.8 %collective-permute-start = (f32[192,1,2,128]{3,2,1,0:T(2,128)S(1)}, f32[192,1,2,128]{3,2,1,0:T(2,128)S(1)}, u32[]{:S(2)}, u32[]{:S(2)}) collective-permute-start(f32[192,1,2,128]{3,2,1,0:T(2,128)S(1)} %get-tuple-element.17), channel_id=1, source_target_pairs={{8,0},{0,8},{9,1},{1,9},{10,2},{2,10},{11,3},{3,11},{12,4},{4,12},... | collective-permute-start | bytes 589832 | tf_op jit(solution)/shard_map/ppermute | solution.py:24
  4.7 9.1 %collective-permute-start.1 = (f32[192,1,2,128]{3,2,1,0:T(2,128)S(1)}, f32[192,1,2,128]{3,2,1,0:T(2,128)S(1)}, u32[]{:S(2)}, u32[]{:S(2)}) collective-permute-start(f32[192,1,2,128]{3,2,1,0:T(2,128)S(1)} %get-tuple-element.16), channel_id=1, source_target_pairs={{0,8},{8,0},{1,9},{9,1},{2,10},{10,2},{3,11},{11,3},{4,12},{12,4},... | collective-permute-start | bytes 589832 | tf_op jit(solution)/shard_map/ppermute | solution.py:21
  6.3 82.5 %collective-permute-start.8 = (f32[1,8,8,2,128]{4,3,2,1,0:T(2,128)}, f32[1,8,8,2,128]{4,3,2,1,0:T(2,128)}, u32[]{:S(2)}, u32[]{:S(2)}) collective-permute-start(f32[1,8,8,2,128]{4,3,2,1,0:T(2,128)} %get-tuple-element.18), channel_id=1, source_target_pairs={{0,16},{1,17},{2,18},{3,19},{4,20},{5,21},{6,22},{7,23},{8,24},{9,... | collective-permute-start | bytes 196616 | tf_op jit(solution)/shard_map/ppermute | solution.py:12
  8.4 80.5 %collective-permute-start.9 = (f32[1,8,8,2,128]{4,3,2,1,0:T(2,128)}, f32[1,8,8,2,128]{4,3,2,1,0:T(2,128)}, u32[]{:S(2)}, u32[]{:S(2)}) collective-permute-start(f32[1,8,8,2,128]{4,3,2,1,0:T(2,128)} %get-tuple-element.19), channel_id=1, source_target_pairs={{16,0},{17,1},{18,2},{19,3},{20,4},{21,5},{22,6},{23,7},{24,8},{25... | collective-permute-start | bytes 196616 | tf_op jit(solution)/shard_map/ppermute | solution.py:12
  10.5 3.4 %copy-start.3 = (f32[192,1,2,128]{3,2,1,0:T(2,128)}, f32[192,1,2,128]{3,2,1,0:T(2,128)S(1)}, u32[]{:S(2)}) copy-start(f32[192,1,2,128]{3,2,1,0:T(2,128)S(1)} %collective-permute-done) | copy-start | bytes 589828
  13.8 0.7 copy-start.5
  16.5 6.4 %copy-start.10 = (f32[6,2]{0,1:T(2,128)S(1)}, f32[6,2]{0,1:T(2,128)}, u32[]{:S(2)}) copy-start(f32[6,2]{0,1:T(2,128)} %param.5) | copy-start | bytes 148
  16.6 7.3 %copy-start = (f32[6,32,8,2,128]{4,3,2,1,0:T(2,128)S(1)}, f32[6,32,8,2,128]{4,3,2,1,0:T(2,128)}, u32[]{:S(2)}) copy-start(f32[6,32,8,2,128]{4,3,2,1,0:T(2,128)} %param.6) | copy-start | bytes 4718596
  18.1 44.1 %collective-permute-start.2 = (f32[192,10,1,128]{3,2,1,0:T(1,128)S(1)}, f32[192,10,1,128]{3,2,1,0:T(1,128)}, u32[]{:S(2)}, u32[]{:S(2)}) collective-permute-start(f32[192,10,1,128]{3,2,1,0:T(1,128)S(1)} %get-tuple-element.4), channel_id=1, source_target_pairs={{1,0},{2,1},{3,2},{4,3},{5,4},{6,5},{7,6},{0,7},{9,8},{10,9},{11,1... | collective-permute-start | bytes 2949128 | tf_op jit(solution)/shard_map/ppermute | solution.py:24
  23.0 39.3 %collective-permute-start.3 = (f32[192,10,1,128]{3,2,1,0:T(1,128)S(1)}, f32[192,10,1,128]{3,2,1,0:T(1,128)}, u32[]{:S(2)}, u32[]{:S(2)}) collective-permute-start(f32[192,10,1,128]{3,2,1,0:T(1,128)S(1)} %get-tuple-element.5), channel_id=1, source_target_pairs={{0,1},{1,2},{2,3},{3,4},{4,5},{5,6},{6,7},{7,0},{8,9},{9,10},{10,1... | collective-permute-start | bytes 2949128 | tf_op jit(solution)/shard_map/ppermute | solution.py:21
  23.1 39.1 %copy-start.8 = (f32[192]{0:T(256)}, f32[192]{0:T(256)S(1)}, u32[]{:S(2)}) copy-start(f32[192]{0:T(256)S(1)} %sub.40) | copy-start | bytes 2308
  26.0 36.3 %copy-start.4 = (f32[192,1,2,128]{3,2,1,0:T(2,128)S(1)}, f32[192,1,2,128]{3,2,1,0:T(2,128)}, u32[]{:S(2)}) copy-start(f32[192,1,2,128]{3,2,1,0:T(2,128)} %copy-done.3) | copy-start | bytes 589828
  26.0 36.3 %copy-start.6 = (f32[192,1,2,128]{3,2,1,0:T(2,128)S(1)}, f32[192,1,2,128]{3,2,1,0:T(2,128)}, u32[]{:S(2)}) copy-start(f32[192,1,2,128]{3,2,1,0:T(2,128)} %copy-done.5) | copy-start | bytes 589828
  62.3 11.3 %copy-start.2 = (f32[6,8,8,2,128]{4,3,2,1,0:T(2,128)S(1)}, f32[6,8,8,2,128]{4,3,2,1,0:T(2,128)}, u32[]{:S(2)}) copy-start(f32[6,8,8,2,128]{4,3,2,1,0:T(2,128)} %param.7) | copy-start | bytes 1179652
  71.5 7.8 %collective-permute-start.4 = (f32[192,1,2,128]{3,2,1,0:T(2,128)S(1)}, f32[192,1,2,128]{3,2,1,0:T(2,128)S(1)}, u32[]{:S(2)}, u32[]{:S(2)}) collective-permute-start(f32[192,1,2,128]{3,2,1,0:T(2,128)S(1)} %get-tuple-element.11), channel_id=1, source_target_pairs={{8,0},{0,8},{9,1},{1,9},{10,2},{2,10},{11,3},{3,11},{12,4},{4,12},... | collective-permute-start | bytes 589832 | tf_op jit(solution)/shard_map/ppermute | solution.py:24
  73.0 9.4 %collective-permute-start.5 = (f32[192,1,2,128]{3,2,1,0:T(2,128)S(1)}, f32[192,1,2,128]{3,2,1,0:T(2,128)S(1)}, u32[]{:S(2)}, u32[]{:S(2)}) collective-permute-start(f32[192,1,2,128]{3,2,1,0:T(2,128)S(1)} %get-tuple-element.10), channel_id=1, source_target_pairs={{0,8},{8,0},{1,9},{9,1},{2,10},{10,2},{3,11},{11,3},{4,12},{12,4},... | collective-permute-start | bytes 589832 | tf_op jit(solution)/shard_map/ppermute | solution.py:21
  86.1 45.1 %collective-permute-start.6 = (f32[192,10,1,128]{3,2,1,0:T(1,128)}, f32[192,10,1,128]{3,2,1,0:T(1,128)}, u32[]{:S(2)}, u32[]{:S(2)}) collective-permute-start(f32[192,10,1,128]{3,2,1,0:T(1,128)} %get-tuple-element.2), channel_id=1, source_target_pairs={{1,0},{2,1},{3,2},{4,3},{5,4},{6,5},{7,6},{0,7},{9,8},{10,9},{11,1... | collective-permute-start | bytes 2949128 | tf_op jit(solution)/shard_map/ppermute | solution.py:24
  88.9 42.3 %collective-permute-start.7 = (f32[192,10,1,128]{3,2,1,0:T(1,128)}, f32[192,10,1,128]{3,2,1,0:T(1,128)}, u32[]{:S(2)}, u32[]{:S(2)}) collective-permute-start(f32[192,10,1,128]{3,2,1,0:T(1,128)} %get-tuple-element.3), channel_id=1, source_target_pairs={{0,1},{1,2},{2,3},{3,4},{4,5},{5,6},{6,7},{7,0},{8,9},{9,10},{10,1... | collective-permute-start | bytes 2949128 | tf_op jit(solution)/shard_map/ppermute | solution.py:21
  95.8 35.3 %copy-start.9 = (f32[192]{0:T(256)S(1)}, f32[192]{0:T(256)}, u32[]{:S(2)}) copy-start(f32[192]{0:T(256)} %copy-done.8) | copy-start | bytes 2308
  141.2 2.6 copy-start.1
  188.8 2.6 copy-start.7
